TPU v7x, 32 devices: a whole 2x2x4 slice. The times are simulated.
32 devices in a mesh: group: 2 (over x), expert: 16 (over z, y, core).
Axes of the slice: x: 2, y: 2, z: 4, core: 2. Of those that a mesh axis runs over, the one named last changes fastest.
Arguments:
- tokens: bfloat16 [4096, 7168], P(('group', 'expert')), parts along dimension 0, may hold values from -6 to 6
- expert_ids: int32 [4096, 2], P(('group', 'expert')), parts along dimension 0, may hold values from 0 to 7, all different within a row; in each aligned block of 128 rows (0 to 127, 128 to 255, ...) at most 64 rows name the same one
- gate_weights: float32 [4096, 2], P(('group', 'expert')), parts along dimension 0, may hold values from 0.05 to 1
- slot_expert: int32 [16], replicated, may hold values from 0 to 7, as said below
- w_gate_up: bfloat16 [16, 7168, 1024], P('expert'), may hold values from -0.0625 to 0.0625
- w_down: bfloat16 [16, 512, 7168], P('expert'), may hold values from -0.1875 to 0.1875
Outputs:
- moe_output: bfloat16 [4096, 7168], P(('group', 'expert')), parts along dimension 0
There are 2 independent parts, one for each index of `group`. A program takes and returns all parts, laid end to end along the dimension named above; an argument that names none is the same for every part. Nothing has to cross between parts.
Inputs may be any that keep to these rules, and one draw needn't show every extreme that they name: `expert_ids`: each token names 2 different experts. In the rows of one device (128 tokens) no expert is named more than 64 times, a bound that some block reaches. `slot_expert`: the first 8 slots hold every expert once, and slot s + 8 holds the same expert as slot s.
All inputs are finite; a program needn't handle non-finite values.
Results may differ from a plain program's by a relative error of at most 0.0065.
Values may be sent and summed in bfloat16 or wider, within the bound.
A program may use at most 128 MiB of HBM per device.

v0:
```python
import jax
import jax.numpy as jnp
from jax import lax
from jax.sharding import PartitionSpec as P


def per_device(tokens, expert_ids, gate_weights, slot_expert, w_gate_up, w_down):
    devices = lax.axis_size("expert")
    half_dev = devices // 2
    tok_rows, model_width = tokens.shape
    top_count = expert_ids.shape[1]
    capacity = 4 * tok_rows * top_count // devices
    flat_ids = expert_ids.reshape(-1)
    expert_range = jnp.arange(half_dev, dtype=jnp.int32)
    onehot = (flat_ids[:, None] == expert_range[None, :]).astype(jnp.int32)
    choice_rank = jnp.sum(jnp.cumsum(onehot, axis=0) * onehot, axis=1) - 1
    lower_expert = slot_expert[:half_dev]
    lower_match = (lower_expert[None, :] == expert_range[:, None]).astype(jnp.int32)
    lower_slot = jnp.sum(lower_match * jnp.arange(half_dev, dtype=jnp.int32)[None, :], axis=1)
    slot_of_choice = jnp.sum(onehot * lower_slot[None, :], axis=1)
    row_index = slot_of_choice * capacity + choice_rank
    target_rows = jnp.arange(half_dev * capacity, dtype=jnp.int32)
    matches = jnp.any(
        row_index.reshape(tok_rows, top_count)[None, :, :] == target_rows[:, None, None], axis=2
    )
    selector = matches.astype(jnp.bfloat16)
    selector = jnp.concatenate([selector, selector], axis=0)
    outgoing = jnp.dot(selector, tokens, preferred_element_type=jnp.float32).astype(jnp.bfloat16)
    outgoing = outgoing.reshape(devices, capacity, model_width)
    gate_up = w_gate_up[0]
    down_proj = w_down[0]
    rows = lax.all_to_all(outgoing, "expert", split_axis=0, concat_axis=0, tiled=True)
    flat_rows = rows.reshape(-1, model_width)
    projected = jnp.dot(flat_rows, gate_up, preferred_element_type=jnp.float32)
    hidden_half = projected.shape[1] // 2
    hidden = (jax.nn.silu(projected[:, :hidden_half]) * projected[:, hidden_half:]).astype(
        jnp.bfloat16
    )
    partial_value = jnp.dot(hidden, down_proj, preferred_element_type=jnp.float32).astype(
        jnp.bfloat16
    )
    returned = lax.all_to_all(
        partial_value.reshape(rows.shape), "expert", split_axis=0, concat_axis=0, tiled=True
    )
    expert_table = (
        returned[:half_dev].astype(jnp.float32) + returned[half_dev:].astype(jnp.float32)
    ).astype(jnp.bfloat16)
    chosen_rows = jnp.take(expert_table.reshape(-1, model_width), row_index, axis=0)
    chosen_rows = chosen_rows.reshape(tok_rows, top_count, model_width)
    total = jnp.sum(gate_weights[:, :, None] * chosen_rows.astype(jnp.float32), axis=1)
    return total.astype(jnp.bfloat16)


def solution(mesh):
    return jax.shard_map(
        per_device,
        mesh=mesh,
        in_specs=(
            P(("group", "expert"), None),
            P(("group", "expert"), None),
            P(("group", "expert"), None),
            P(),
            P("expert", None, None),
            P("expert", None, None),
        ),
        out_specs=P(("group", "expert"), None),
        check_vma=False,
    )
```

profile of v0, /device:TPU:13, one launch (start us, length us, event | category | flops | bytes accessed | tf_op | source)
XLA Modules:
  0.0 734.6 jit_solution(14149827424566211441)
XLA Ops:
  0.0 0.0 copy-start
  0.0 0.9 copy.12
  0.9 0.1 eq.58
  1.1 0.1 eq.51
  1.2 0.6 reduce-window.6
  1.8 0.2 slice_reduce_fusion
  2.1 0.8 select_reduce_fusion.1
  2.8 0.1 select_reduce_fusion
  2.9 0.1 add.70
  3.1 0.1 copy.14
  3.1 0.1 fusion.6
  3.2 0.0 copy-done
  3.2 7.8 %convolution_convert_fusion.1 = bf16[1024,7168]{1,0:T(8,128)(2,1)} fusion(bf16[128,7168]{1,0:T(8,128)(2,1)S(1)} %copy-done, pred[512,128]{1,0:T(8,128)(4,1)S(1)} %fusion.6), kind=kOutput, calls=%fused_computation.5 | convolution fusion | flops 1886519296 | bytes 16580608 | tf_op jit(solution)/shard_map/dot_general | solution.py:28
  11.0 0.0 copy-start.3
  11.0 323.7 %all_to_all.10 = bf16[16,64,7168]{2,1,0:T(8,128)(2,1)S(1)} all-to-all(bf16[16,64,7168]{2,1,0:T(8,128)(2,1)} %bitcast.22), channel_id=1, replica_groups=mesh['group'=2,'expert'=16] {'expert'}, dimensions={0} | all-to-all | bytes 29360128 | tf_op jit(solution)/shard_map/all_to_all | solution.py:32
  334.7 0.0 copy-done.3
  334.7 16.8 %fusion = f32[1024,1024]{1,0:T(8,128)} fusion(bf16[1024,7168]{1,0:T(8,128)(2,1)S(1)} %bitcast.24, bf16[1,7168,1024]{2,1,0:T(8,128)(2,1)S(1)} %copy-done.3), kind=kOutput, calls=%fused_computation.1 | convolution fusion | flops 15032385536 | bytes 33554432 | tf_op jit(solution)/shard_map/dot_general | solution.py:34
  351.6 14.3 %convolution_convert_fusion = bf16[1024,7168]{1,0:T(8,128)(2,1)} fusion(bf16[1,512,7168]{2,1,0:T(8,128)(2,1)} %param.11, f32[1024,1024]{1,0:T(8,128)} %fusion), kind=kOutput, calls=%fused_computation.4 | convolution fusion | flops 7526678528 | bytes 26214400 | tf_op jit(solution)/shard_map/dot_general | solution.py:39
  365.9 0.0 copy-start.2
  365.9 6.4 all-to-all-start.1
  372.2 0.0 copy-done.2
  372.2 0.1 copy.11
  372.4 317.0 %all-to-all-done.1 = bf16[16,64,7168]{2,1,0:T(8,128)(2,1)} async-done(((bf16[16,64,7168]{2,1,0:T(8,128)(2,1)}), bf16[16,64,7168]{2,1,0:T(8,128)(2,1)}, u32[]{:S(2)}, u32[]{:S(2)}) %all-to-all-start.1) | async-done | bytes 14680096 | tf_op jit(solution)/shard_map/all_to_all | solution.py:42
  689.4 10.9 %add_convert_fusion = bf16[8,64,7168]{2,1,0:T(8,128)(2,1)} fusion(bf16[16,64,7168]{2,1,0:T(8,128)(2,1)} %all-to-all-done.1), kind=kLoop, calls=%fused_computation.3 | loop fusion | flops 14680064 | bytes 22020096 | tf_op jit(solution)/shard_map/convert_element_type | solution.py:47
  700.4 0.0 copy-start.1
  700.4 12.2 %gather_fusion = bf16[256,7168]{1,0:T(8,128)(2,1)} fusion(bf16[512,7168]{1,0:T(8,128)(2,1)} %bitcast.21, s32[1024]{0:T(1024)S(1)} %pad_clamp_fusion), kind=kCustom, calls=%fused_computation | custom fusion | bytes 7341056 | tf_op jit(solution)/shard_map/jit(_take)/gather | solution.py:48
  712.5 8.1 %gather.7 = bf16[128,2,7168]{2,1,0:T(2,128)(2,1)} reshape(bf16[256,7168]{1,0:T(8,128)(2,1)} %gather_fusion) | data formatting | bytes 7340032 | tf_op jit(solution)/shard_map/jit(_take)/gather | solution.py:48
  720.7 14.0 %multiply_reduce_fusion = bf16[128,7168]{1,0:T(8,128)(2,1)} fusion(bf16[128,2,7168]{2,1,0:T(2,128)(2,1)} %gather.7, pred[128,2]{1,0:T(8,128)(4,1)S(1)} %compare_and_fusion, f32[128,2]{1,0:T(8,128)S(1)} %copy.11), kind=kLoop, calls=%fused_computation.7 | loop fusion | flops 6422528 | bytes 5506304 | tf_op jit(solution)/shard_map/reduce_sum | solution.py:50
  734.6 0.0 copy-done.1
  (7 shorter events, 0.1 us)
Async XLA Ops:
  0.0 3.2 copy-start
  11.0 323.7 %copy-start.3 = (bf16[1,7168,1024]{2,1,0:T(8,128)(2,1)S(1)}, bf16[1,7168,1024]{2,1,0:T(8,128)(2,1)}, u32[]{:S(2)}) copy-start(bf16[1,7168,1024]{2,1,0:T(8,128)(2,1)} %param.10) | copy-start | bytes 44040196
  365.9 6.4 copy-start.2
  365.9 323.5 %all-to-all-start.1 = ((bf16[16,64,7168]{2,1,0:T(8,128)(2,1)}), bf16[16,64,7168]{2,1,0:T(8,128)(2,1)}, u32[]{:S(2)}, u32[]{:S(2)}) async-start(bf16[16,64,7168]{2,1,0:T(8,128)(2,1)} %bitcast.23), calls=%async_computation.1 | async-start | bytes 29360128 | tf_op jit(solution)/shard_map/all_to_all | solution.py:42
  700.4 34.2 %copy-start.1 = (bf16[128,7168]{1,0:T(8,128)(2,1)S(1)}, bf16[128,7168]{1,0:T(8,128)(2,1)}, u32[]{:S(2)}) copy-start(bf16[128,7168]{1,0:T(8,128)(2,1)} %param.6) | copy-start | bytes 5505028
where the time goes:
time: 735 us
  blocking collectives  324 us (44%)
  waiting for transfers between devices  317 us (43%)
  matrix products  38.9 us (5%)
  other arithmetic  26.5 us (4%)
  local copies, waits for them, and re-layouts  22 us (3%)
    all_to_all x1, blocking collectives, per_device(): lax.all_to_all(outgoing, 'expert', split_axis=0, concat_axis=0, tiled=True)  324 us
    all_to_all x1, waiting for transfers between devices, per_device(): lax.all_to_all(partial_value.reshape(rows.shape), 'expert', split_axis=0,...  317 us
    gather x2, local copies, waits for them, and re-layouts, per_device(): jnp.take(expert_table.reshape(-1, model_width), row_index, axis=0)  20.3 us
    dot_general x1, matrix products, per_device(): projected = jnp.dot(flat_rows, gate_up, preferred_element_type=jnp.float32)  16.8 us
  transfers between devices with their start and end apart: 1, of which 1 were waited for; matrix products, arithmetic and copies ran while one was open for 0% of the time, Pallas kernels for 0%

commit v1 on v0

v1 whole, which is shorter than its diff:
```python
import jax
import jax.numpy as jnp
from jax import lax
from jax.sharding import PartitionSpec as P

CHUNKS = 1


def per_device(tokens, expert_ids, gate_weights, slot_expert, w_gate_up, w_down):
    devices = lax.axis_size("expert")
    experts = devices // 2
    rows, width = tokens.shape
    half = w_down.shape[1]
    chosen = expert_ids[:, :, None] == slot_expert[None, None, :experts]
    weights = jnp.sum(jnp.where(chosen, gate_weights[:, :, None], 0.0), axis=1)
    all_weights = lax.all_gather(weights, "expert", axis=0, tiled=False)
    column = lax.rem(lax.axis_index("expert"), experts)
    mine = lax.dynamic_index_in_dim(all_weights, column, axis=2, keepdims=False)
    step = rows // CHUNKS
    out = []
    for c in range(CHUNKS):
        part = lax.all_gather(tokens[c * step:(c + 1) * step], "expert", axis=0, tiled=True)
        w = mine[:, c * step:(c + 1) * step].reshape(-1, 1)
        projected = jnp.dot(part, w_gate_up[0], preferred_element_type=jnp.float32)
        hidden = jax.nn.silu(projected[:, :half]) * projected[:, half:] * w
        partial = jnp.dot(hidden.astype(jnp.bfloat16), w_down[0], preferred_element_type=jnp.float32).astype(jnp.bfloat16)
        out.append(lax.psum_scatter(partial, "expert", scatter_dimension=0, tiled=True))
    return jnp.concatenate(out, axis=0)


def solution(mesh):
    return jax.shard_map(
        per_device,
        mesh=mesh,
        in_specs=(
            P(("group", "expert"), None),
            P(("group", "expert"), None),
            P(("group", "expert"), None),
            P(),
            P("expert", None, None),
            P("expert", None, None),
        ),
        out_specs=P(("group", "expert"), None),
        check_vma=False,
    )
```

time: 735 us -> 510 us (0.69)
  blocking collectives: 324 us -> 16 us
  waiting for transfers between devices: 317 us -> 413 us
  other arithmetic: 26.5 us -> 0.77 us
  matrix products: 38.9 us -> 62.5 us
  local copies, waits for them, and re-layouts: 22 us -> 0.01 us
  between operations: 0.08 us -> 13.4 us
    all_to_all x1 -> x0, blocking collectives: 324 us -> none  [per_device(): lax.all_to_all(outgoing, 'expert', split_axis=0, concat_axis=0, tiled=True)]
    all_to_all x1 -> x0, waiting for transfers between devices: 317 us -> none  [per_device(): lax.all_to_all(partial_value.reshape(rows.shape), 'expert', split_axis=0,...]
    reduce_scatter x0 -> x1, waiting for transfers between devices: none -> 278 us  [per_device(): lax.psum_scatter(partial, 'expert', scatter_dimension=0, tiled=True)]
    all_gather x0 -> x1, waiting for transfers between devices: none -> 135 us  [per_device(): lax.all_gather(tokens[c * step:(c + 1) * step], 'expert', axis=0, tiled=T...]
    dot_general x3 -> x2, matrix products: 38.9 us -> 62.5 us  [the longest x1 38.3 us: per_device(): projected = jnp.dot(part, w_gate_up[0], preferred_element_type=jnp.float32)]
    gather x2 -> x0, local copies, waits for them, and re-layouts: 20.3 us -> none  [per_device(): jnp.take(expert_table.reshape(-1, model_width), row_index, axis=0)]
    all_gather x0 -> x1, blocking collectives: none -> 16 us  [per_device(): all_weights = lax.all_gather(weights, 'expert', axis=0, tiled=False)]
    reduce_sum x3 -> x1, other arithmetic: 14.8 us -> 0.77 us  [per_device(): weights = jnp.sum(jnp.where(chosen, gate_weights[:, :, None], 0.0), axis=1)]
  transfers between devices with their start and end apart: 1 -> 2, of which waited for: 1 -> 2; matrix products, arithmetic and copies ran while one was open for 0% -> 0% of each run, Pallas kernels for 0% -> 0%
where the time goes in v1:
time: 510 us; the launch traced here: 506 us
  waiting for transfers between devices  413 us (81%)
  matrix products  62.5 us (12%)
  blocking collectives  16 us (3%)
  between operations  13.4 us (3%)
    reduce_scatter x1, waiting for transfers between devices, per_device(): lax.psum_scatter(partial, 'expert', scatter_dimension=0, tiled=True)  278 us
    all_gather x1, waiting for transfers between devices, per_device(): lax.all_gather(tokens[c * step:(c + 1) * step], 'expert', axis=0, tiled=T...  135 us
    dot_general x1, matrix products, per_device(): projected = jnp.dot(part, w_gate_up[0], preferred_element_type=jnp.float32)  38.3 us
    dot_general x1, matrix products, per_device(): jnp.dot(hidden.astype(jnp.bfloat16), w_down[0], preferred_element_type=jn...  24.2 us
    all_gather x1, blocking collectives, per_device(): all_weights = lax.all_gather(weights, 'expert', axis=0, tiled=False)  16 us
  transfers between devices with their start and end apart: 2, of which 2 were waited for; matrix products, arithmetic and copies ran while one was open for 0% of the time, Pallas kernels for 0%

profile of v1, /device:TPU:13, one launch (start us, length us, event | category | flops | bytes accessed | tf_op | source)
XLA Modules:
  0.0 506.2 jit_solution(5771733906057629192)
XLA Ops:
  6.5 0.0 all-gather.3.cloned.1.call-start
  6.5 0.7 all-gather.3.cloned.1.call-update
  7.3 0.0 reduce-scatter.2.cloned.1.call-start
  7.3 0.8 select_reduce_fusion
  8.1 16.0 %all-gather = f32[2048,8]{0,1:T(8,128)S(1)} all-gather(f32[128,8]{0,1:T(8,128)S(1)} %select_reduce_fusion), channel_id=2, replica_groups=mesh['group'=2,'expert'=16] {'expert'}, dimensions={0}, use_global_device_ids=true | all-gather | bytes 69632 | tf_op jit(solution)/shard_map/all_gather | solution.py:16
  24.1 134.6 %all-gather.3.cloned.1.call-done = bf16[2048,7168]{1,0:T(8,128)(2,1)} async-done(((bf16[128,7168]{1,0:T(8,128)(2,1)}), bf16[2048,7168]{1,0:T(8,128)(2,1)}) %all-gather.3.cloned.1.call-update) | async-done | bytes 29360144 | tf_op jit(solution)/shard_map/all_gather | solution.py:22
  158.7 38.3 %fusion = f32[2048,1024]{1,0:T(8,128)} fusion(bf16[2048,7168]{1,0:T(8,128)(2,1)} %all-gather.3.cloned.1.call-done, bf16[1,7168,1024]{2,1,0:T(8,128)(2,1)} %param.10), kind=kOutput, calls=%fused_computation.1 | convolution fusion | flops 30064771072 | bytes 52428800 | tf_op jit(solution)/shard_map/dot_general | solution.py:24
  197.0 24.2 %convolution_convert_fusion = bf16[2048,7168]{1,0:T(8,128)(2,1)} fusion(bf16[1,512,7168]{2,1,0:T(8,128)(2,1)} %param.11, f32[2048,1024]{1,0:T(8,128)} %fusion, f32[2048]{0:T(1024)S(1)} %bitcast.13), kind=kOutput, calls=%fused_computation | convolution fusion | flops 15054405632 | bytes 45096960 | tf_op jit(solution)/shard_map/dot_general | solution.py:26
  221.2 0.0 reduce-scatter.2.cloned.1.call-update
  221.2 278.1 %reduce-scatter.2.cloned.1.call-done = bf16[128,7168]{1,0:T(8,128)(2,1)} async-done(((bf16[2048,7168]{1,0:T(8,128)(2,1)}), bf16[128,7168]{1,0:T(8,128)(2,1)}) %reduce-scatter.2.cloned.1.call-update) | async-done | bytes 1835024 | tf_op jit(solution)/shard_map/reduce_scatter | solution.py:27
  (1 shorter events, 0.0 us)
Async XLA Ops:
  6.5 152.1 %all-gather.3.cloned.1.call-start = ((), (), s32[]{:S(2)}) async-start(), calls=%async_computation.1 | async-start | bytes 31195136 | tf_op jit(solution)/shard_map/all_gather | solution.py:22
  7.3 492.1 %reduce-scatter.2.cloned.1.call-start = ((), (), s32[]{:S(2)}) async-start(), calls=%async_computation.2 | async-start | bytes 31195136 | tf_op jit(solution)/shard_map/reduce_scatter | solution.py:27
Sparse Core Ops, SparseCore 0:
  8.9 149.6 all-gather.2
  221.3 277.9 reduce-scatter.1
